TPU v7x, 512 devices: a whole 4x8x8 slice. The times are simulated.
512 devices in a mesh: feat: 32 (over x, z), tok: 16 (over y, core).
Axes of the slice: x: 4, y: 8, z: 8, core: 2. Of those that a mesh axis runs over, the one named last changes fastest.
Arguments:
- activations: bfloat16 [2048, 8192], P('tok', 'feat'), may hold values from -6 to 6
- w_base: bfloat16 [8192, 8192], P('feat', 'tok'), may hold values from -0.0625 to 0.0625
- blk_vals: bfloat16 [96, 128, 128], P('feat'), may hold values from -0.5 to 0.5
- blk_index: int32 [96, 2], P('feat'), may hold values from 0 to 63, as said below
- blk_count: int32 [32], P('feat'), may hold values from 1 to 3, as said below
- a_down: bfloat16 [8192, 64], P('feat'), may hold values from -0.0625 to 0.0625
- b_up: bfloat16 [64, 8192], P(None, 'feat'), may hold values from -0.75 to 0.75
- grad_out: bfloat16 [2048, 8192], P('tok', 'feat'), may hold values from -6 to 6
Outputs:
- projected: bfloat16 [2048, 8192], P('tok', 'feat')
- grad_x: bfloat16 [2048, 8192], P('tok', 'feat')
- grad_blocks: float32 [96, 128, 128], P('feat')
- grad_a: float32 [8192, 64], P('feat')
- grad_b: float32 [64, 8192], P(None, 'feat')
Inputs may be any that keep to these rules, and one draw needn't show every extreme that they name: `blk_index`: column 0 is below 2 and column 1 below 64; both largest values occur in every draw. `blk_count`: some feature shard holds exactly 3 live slots in every draw.
All inputs are finite; a program needn't handle non-finite values.
Results may differ from a plain program's by a relative error of at most 0.014.
Values may be sent and summed in bfloat16 or wider, within the bound.
A program may use at most 64 MiB of HBM per device.

v0:
```python
import jax
import jax.numpy as jnp
from jax import lax
from jax.sharding import PartitionSpec as P

BLK = 128


def on_device(activations, w_base, blk_vals, blk_index, blk_count, a_down, b_up, grad_out):
    tok_rows = activations.shape[0]
    grad_scale = float(tok_rows * lax.axis_size("tok")) ** (-0.5)
    live_count = blk_count[0]
    u_part = jnp.dot(activations, a_down, preferred_element_type=jnp.float32)
    v_part = jnp.dot(grad_out, b_up.T, preferred_element_type=jnp.float32)
    u_total = lax.psum(u_part, "feat")
    u_half = u_total.astype(jnp.bfloat16)
    w_rows = lax.all_gather(w_base, "tok", axis=1, tiled=True)
    partial_value = jnp.dot(activations, w_rows, preferred_element_type=jnp.float32)
    for slot_idx in range(blk_vals.shape[0]):
        is_live = (slot_idx < live_count).astype(jnp.float32)
        row_start = blk_index[slot_idx, 0] * BLK
        col_start = blk_index[slot_idx, 1] * BLK
        x_cols = lax.dynamic_slice_in_dim(activations, row_start, BLK, 1)
        forward_add = (
            jnp.dot(x_cols, blk_vals[slot_idx], preferred_element_type=jnp.float32) * is_live
        )
        current = lax.dynamic_slice_in_dim(partial_value, col_start, BLK, 1)
        partial_value = lax.dynamic_update_slice_in_dim(
            partial_value, current + forward_add, col_start, 1
        )
    own_sums = lax.psum_scatter(
        partial_value.astype(jnp.bfloat16), "feat", scatter_dimension=1, tiled=True
    ).astype(jnp.float32)
    projected = (own_sums + jnp.dot(u_half, b_up, preferred_element_type=jnp.float32)).astype(
        jnp.bfloat16
    )
    v_total = lax.psum(v_part, "feat")
    v_half = v_total.astype(jnp.bfloat16)
    cot_rows = lax.all_gather(grad_out, "feat", axis=1, tiled=True)
    backward = jnp.dot(cot_rows, w_rows.T, preferred_element_type=jnp.float32)
    block_terms = []
    for slot_idx in range(blk_vals.shape[0]):
        is_live = (slot_idx < live_count).astype(jnp.float32)
        row_start = blk_index[slot_idx, 0] * BLK
        col_start = blk_index[slot_idx, 1] * BLK
        x_cols = lax.dynamic_slice_in_dim(activations, row_start, BLK, 1)
        g_cols = lax.dynamic_slice_in_dim(cot_rows, col_start, BLK, 1)
        back_add = (
            jnp.dot(g_cols, blk_vals[slot_idx].T, preferred_element_type=jnp.float32) * is_live
        )
        current = lax.dynamic_slice_in_dim(backward, row_start, BLK, 1)
        backward = lax.dynamic_update_slice_in_dim(backward, current + back_add, row_start, 1)
        block_terms.append(jnp.dot(x_cols.T, g_cols, preferred_element_type=jnp.float32) * is_live)
    grad_x = (backward + jnp.dot(v_half, a_down.T, preferred_element_type=jnp.float32)).astype(
        jnp.bfloat16
    )
    block_local = jnp.stack(block_terms, axis=0)
    down_local = jnp.dot(activations.T, v_half, preferred_element_type=jnp.float32)
    up_local = jnp.dot(u_half.T, grad_out, preferred_element_type=jnp.float32)
    block_sum, down_sum, up_sum = lax.psum((block_local, down_local, up_local), "tok")
    return (projected, grad_x, block_sum * grad_scale, down_sum * grad_scale, up_sum * grad_scale)


def solution(mesh):
    in_specs = (
        P("tok", "feat"),
        P("feat", "tok"),
        P("feat", None, None),
        P("feat", None),
        P("feat"),
        P("feat", None),
        P(None, "feat"),
        P("tok", "feat"),
    )
    out_specs = (
        P("tok", "feat"),
        P("tok", "feat"),
        P("feat", None, None),
        P("feat", None),
        P(None, "feat"),
    )
    return jax.shard_map(
        on_device, mesh=mesh, in_specs=in_specs, out_specs=out_specs, check_vma=False
    )
```

profile of v0, /device:TPU:8, one launch (start us, length us, event | category | flops | bytes accessed | tf_op | source)
XLA Modules:
  0.0 517.7 jit_solution(15335018569101038187)
XLA Ops:
  7.2 0.0 copy-start
  7.2 0.0 all-gather.5.cloned.1.call-start
  7.2 0.7 all-gather.5.cloned.1.call-update
  7.9 0.0 all-gather.3.cloned.1.call-start
  8.0 0.7 all-gather.3.cloned.1.call-update
  8.7 0.0 all-reduce.4.cloned.1.call-start
  8.7 1.6 fusion.55
  14.9 1.0 fusion.59
  15.9 0.0 copy-done
  15.9 0.9 fusion.57
  16.8 149.2 %all-reduce = (bf16[128,64]{0,1:T(8,128)(2,1)S(1)}, bf16[128,64]{0,1:T(8,128)(2,1)S(1)}) all-reduce(f32[128,64]{0,1:T(8,128)S(1)} %fusion.57, f32[128,64]{0,1:T(8,128)S(1)} %fusion.59), channel_id=1, replica_groups=mesh['feat'=32,'tok'=16] {'feat'}, use_global_device_ids=true, to_apply=%region_1.0 | all-reduce | flops 16384 | bytes 98304 | tf_op jit(solution)/shard_map/psum | solution.py:15
  165.9 1.6 fusion.60
  167.6 0.8 convolution_bitcast_fusion
  168.3 0.0 all-gather.5.cloned.1.call-done
  168.3 0.9 fusion.2
  169.3 0.9 fusion.3
  170.2 0.9 fusion.4
  171.2 0.7 pad_maximum_fusion
  171.9 0.0 all-reduce.4.cloned.1.call-update
  171.9 0.0 copy-start.2
  171.9 0.0 reduce-scatter.2.cloned.1.call-start
  172.0 0.0 all-gather.3.cloned.1.call-done
  172.0 2.9 fusion.56
  174.9 0.0 copy-done.2
  174.9 0.1 fusion.16
  175.1 0.1 fusion.14
  175.2 0.1 fusion.12
  175.3 0.0 copy-start.1
  175.3 1.6 convert_element_type.45
  176.9 0.0 reduce-scatter.2.cloned.1.call-update
  177.0 0.0 copy-start.3
  177.0 0.0 copy-start.4
  177.0 101.2 %all-reduce.4.cloned.1.call-done = (f32[3,128,128]{2,1,0:T(8,128)}, f32[256,64]{0,1:T(8,128)}, f32[64,256]{1,0:T(8,128)}) async-done(((f32[3,128,128]{2,1,0:T(8,128)}, f32[256,64]{0,1:T(8,128)}, f32[64,256]{1,0:T(8,128)}), (f32[3,128,128]{2,1,0:T(8,128)}, f32[256,64]{0,1:T(8,128)}, f32[64,256]{1,0:T(8,128)})) %all-reduce.4.cloned.1.call-update) | async-done | bytes 327696 | tf_op jit(solution)/shard_map/psum | solution.py:60
  278.2 1.5 broadcast_multiply_fusion.2
  279.7 1.5 broadcast_multiply_fusion.1
  281.2 1.6 broadcast_multiply_fusion
  282.8 0.0 copy-done.1
  282.8 3.7 fusion.58
  286.5 0.1 fusion.10
  286.6 0.2 fusion.8
  286.8 0.2 fusion.6
  287.0 0.0 copy-done.3
  287.0 0.8 fusion.1
  287.8 221.7 %reduce-scatter.2.cloned.1.call-done = bf16[128,256]{1,0:T(8,128)(2,1)} async-done(((bf16[128,8192]{1,0:T(8,128)(2,1)}), bf16[128,256]{1,0:T(8,128)(2,1)}) %reduce-scatter.2.cloned.1.call-update) | async-done | bytes 65552 | tf_op jit(solution)/shard_map/reduce_scatter | solution.py:31
  509.5 0.0 copy-done.4
  509.5 1.7 fusion
Async XLA Ops:
  7.2 8.7 %copy-start = (bf16[128,256]{1,0:T(8,128)(2,1)S(1)}, bf16[128,256]{1,0:T(8,128)(2,1)}, u32[]{:S(2)}) copy-start(bf16[128,256]{1,0:T(8,128)(2,1)} %param.8) | copy-start | bytes 196612
  7.2 161.1 %all-gather.5.cloned.1.call-start = ((), (), s32[]{:S(2)}) async-start(), calls=%async_computation.3 | async-start | bytes 2162688 | tf_op jit(solution)/shard_map/all_gather | solution.py:39
  7.9 164.1 %all-gather.3.cloned.1.call-start = ((), (), s32[]{:S(2)}) async-start(), calls=%async_computation.1 | async-start | bytes 4456448 | tf_op jit(solution)/shard_map/all_gather | solution.py:17
  8.7 269.5 %all-reduce.4.cloned.1.call-start = ((), (), s32[]{:S(2)}) async-start(), calls=%async_computation.4 | async-start | bytes 655360 | tf_op jit(solution)/shard_map/psum | solution.py:60
  171.9 3.0 copy-start.2
  171.9 337.6 %reduce-scatter.2.cloned.1.call-start = ((), (), s32[]{:S(2)}) async-start(), calls=%async_computation.2 | async-start | bytes 2162688 | tf_op jit(solution)/shard_map/reduce_scatter | solution.py:31
  175.3 107.4 %copy-start.1 = (bf16[128,8192]{1,0:T(8,128)(2,1)S(1)}, bf16[128,8192]{1,0:T(8,128)(2,1)}, u32[]{:S(2)}) copy-start(bf16[128,8192]{1,0:T(8,128)(2,1)} %all-gather.5.cloned.1.call-done) | copy-start | bytes 6291460
  177.0 110.0 %copy-start.3 = (bf16[256,64]{0,1:T(8,128)(2,1)S(1)}, bf16[256,64]{0,1:T(8,128)(2,1)}, u32[]{:S(2)}) copy-start(bf16[256,64]{0,1:T(8,128)(2,1)} %param.13) | copy-start | bytes 98308
  177.0 332.5 %copy-start.4 = (bf16[64,256]{1,0:T(8,128)(2,1)S(1)}, bf16[64,256]{1,0:T(8,128)(2,1)}, u32[]{:S(2)}) copy-start(bf16[64,256]{1,0:T(8,128)(2,1)} %param.14) | copy-start | bytes 98308
Sparse Core Ops, SparseCore 0:
  11.0 85.3 all-gather.4
  98.6 43.1 all-gather.2
  172.0 106.1 all-reduce.3
  282.5 226.9 reduce-scatter.1
where the time goes:
time: 518 us
  waiting for transfers between devices  324 us (63%)
  blocking collectives  149 us (29%)
  between operations  18.5 us (4%)
  matrix products  17.1 us (3%)
  other arithmetic  6.85 us (1%)
    reduce_scatter x1, waiting for transfers between devices, on_device(): lax.psum_scatter(partial_value.astype(jnp.bfloat16), 'feat', scatter_dime...  222 us
    psum x1, blocking collectives, on_device(): u_total = lax.psum(u_part, 'feat')  149 us
    psum x1, waiting for transfers between devices, on_device(): lax.psum((block_local, down_local, up_local), 'tok')  101 us
  transfers between devices with their start and end apart: 4, of which 2 were waited for; matrix products, arithmetic and copies ran while one was open for 5% of the time, Pallas kernels for 0%

commit v1 on v0

--- a/solution.py
+++ b/solution.py
@@ -12,7 +12,9 @@
     live_count = blk_count[0]
     u_part = jnp.dot(activations, a_down, preferred_element_type=jnp.float32)
     v_part = jnp.dot(grad_out, b_up.T, preferred_element_type=jnp.float32)
-    u_total = lax.psum(u_part, "feat")
+    u_total = u_part
+    for hop in (1, 2, 4, 8, 16):
+        u_total = u_total + lax.ppermute(u_total, "feat", [(dev, dev ^ hop) for dev in range(32)])
     u_half = u_total.astype(jnp.bfloat16)
     w_rows = lax.all_gather(w_base, "tok", axis=1, tiled=True)
     partial_value = jnp.dot(activations, w_rows, preferred_element_type=jnp.float32)

time: 518 us -> 543 us (1.048)
  starting transfers between devices: 0.16 us -> 23.6 us
  waiting for transfers between devices: 324 us -> 334 us
  blocking collectives: 149 us -> 140 us
    ppermute x0 -> x5, starting transfers between devices: none -> 23.5 us  [on_device(): lax.ppermute(u_total, 'feat', [(dev, dev ^ hop) for dev in range(32)])]
    psum x1, blocking collectives: 149 us -> 140 us  [on_device(): v_total = lax.psum(v_part, 'feat')]
    ppermute x0 -> x5, waiting for transfers between devices: none -> 6.87 us  [on_device(): lax.ppermute(u_total, 'feat', [(dev, dev ^ hop) for dev in range(32)])]
  transfers between devices with their start and end apart: 4 -> 9, of which waited for: 2 -> 5; matrix products, arithmetic and copies ran while one was open for 5% -> 4% of each run, Pallas kernels for 0% -> 0%
where the time goes in v1:
time: 543 us; the launch traced here: 542 us
  waiting for transfers between devices  334 us (62%)
  blocking collectives  140 us (26%)
  starting transfers between devices  23.6 us (4%)
  between operations  18.4 us (3%)
  matrix products  17.1 us (3%)
  other arithmetic  6.9 us (1%)
    reduce_scatter x1, waiting for transfers between devices, on_device(): lax.psum_scatter(partial_value.astype(jnp.bfloat16), 'feat', scatter_dime...  222 us
    psum x1, blocking collectives, on_device(): v_total = lax.psum(v_part, 'feat')  140 us
    psum x1, waiting for transfers between devices, on_device(): lax.psum((block_local, down_local, up_local), 'tok')  105 us
    ppermute x5, starting transfers between devices, on_device(): lax.ppermute(u_total, 'feat', [(dev, dev ^ hop) for dev in range(32)])  23.5 us
  transfers between devices with their start and end apart: 9, of which 5 were waited for; matrix products, arithmetic and copies ran while one was open for 4% of the time, Pallas kernels for 0%

profile of v1, /device:TPU:8, one launch (start us, length us, event | category | flops | bytes accessed | tf_op | source)
XLA Modules:
  0.0 542.4 jit_solution(10395596056023935797)
XLA Ops:
  7.2 0.0 copy-start
  7.2 0.0 all-gather.5.cloned.1.call-start
  7.2 0.7 all-gather.5.cloned.1.call-update
  7.9 0.0 all-gather.3.cloned.1.call-start
  8.0 0.7 all-gather.3.cloned.1.call-update
  8.7 0.0 all-reduce.3.cloned.1.call-start
  8.7 0.9 fusion.54
  9.6 4.3 collective-permute-start
  13.9 1.9 collective-permute-done
  15.8 6.1 %collective-permute-start.1 = (f32[128,64]{0,1:T(8,128)S(1)}, f32[128,64]{0,1:T(8,128)S(1)}, u32[]{:S(2)}, u32[]{:S(2)}) collective-permute-start(f32[128,64]{0,1:T(8,128)S(1)} %add.91), channel_id=1, source_target_pairs={{0,32},{16,48},{32,0},{48,16},{64,96},{80,112},{96,64},{112,80},{1... | collective-permute-start | bytes 98312 | tf_op jit(solution)/shard_map/ppermute | solution.py:17
  21.9 1.9 collective-permute-done.1
  23.8 9.3 %collective-permute-start.2 = (f32[128,64]{0,1:T(8,128)S(1)}, f32[128,64]{0,1:T(8,128)S(1)}, u32[]{:S(2)}, u32[]{:S(2)}) collective-permute-start(f32[128,64]{0,1:T(8,128)S(1)} %add.92), channel_id=1, source_target_pairs={{0,64},{16,80},{32,96},{48,112},{64,0},{80,16},{96,32},{112,48},{1... | collective-permute-start | bytes 98312 | tf_op jit(solution)/shard_map/ppermute | solution.py:17
  33.1 1.0 fusion.56
  34.0 140.3 %psum.28 = bf16[128,64]{0,1:T(8,128)(2,1)S(1)} all-reduce(f32[128,64]{0,1:T(8,128)S(1)} %fusion.56), channel_id=1, replica_groups=mesh['feat'=32,'tok'=16] {'feat'}, use_global_device_ids=true, to_apply=%region_1.0 | all-reduce | flops 8192 | bytes 49152 | tf_op jit(solution)/shard_map/psum | solution.py:39
  174.4 1.9 collective-permute-start.3
  176.3 0.8 convolution_bitcast_fusion
  177.1 3.1 collective-permute-done.3
  180.2 1.9 collective-permute-start.4
  182.1 1.5 fusion.52
  188.1 1.6 fusion.57
  189.7 0.9 fusion.2
  190.7 0.9 fusion.3
  191.6 0.9 fusion.4
  192.6 0.7 pad_maximum_fusion
  193.3 0.0 all-reduce.3.cloned.1.call-update
  193.3 0.0 copy-start.2
  193.3 0.0 reduce-scatter.2.cloned.1.call-start
  193.4 0.0 all-gather.3.cloned.1.call-done
  193.4 2.9 fusion.53
  196.3 0.1 fusion.16
  196.5 0.1 fusion.14
  196.6 0.1 fusion.12
  196.7 0.0 copy-start.1
  196.8 1.6 convert_element_type.45
  198.4 0.0 reduce-scatter.2.cloned.1.call-update
  198.4 0.0 copy-start.3
  198.4 104.5 %all-reduce.3.cloned.1.call-done = (f32[3,128,128]{2,1,0:T(8,128)}, f32[256,64]{0,1:T(8,128)}, f32[64,256]{1,0:T(8,128)}) async-done(((f32[3,128,128]{2,1,0:T(8,128)}, f32[256,64]{0,1:T(8,128)}, f32[64,256]{1,0:T(8,128)}), (f32[3,128,128]{2,1,0:T(8,128)}, f32[256,64]{0,1:T(8,128)}, f32[64,256]{1,0:T(8,128)})) %all-reduce.3.cloned.1.call-update) | async-done | bytes 327696 | tf_op jit(solution)/shard_map/psum | solution.py:62
  302.9 1.5 broadcast_multiply_fusion.2
  304.4 1.5 broadcast_multiply_fusion.1
  305.9 1.6 broadcast_multiply_fusion
  307.5 3.7 fusion.55
  311.2 0.1 fusion.10
  311.4 0.2 fusion.8
  311.5 0.2 fusion.6
  311.7 0.0 copy-done.3
  311.7 0.8 fusion.1
  312.5 221.7 %reduce-scatter.2.cloned.1.call-done = bf16[128,256]{1,0:T(8,128)(2,1)} async-done(((bf16[128,8192]{1,0:T(8,128)(2,1)}), bf16[128,256]{1,0:T(8,128)(2,1)}) %reduce-scatter.2.cloned.1.call-update) | async-done | bytes 65552 | tf_op jit(solution)/shard_map/reduce_scatter | solution.py:33
  534.2 1.7 fusion
  (13 shorter events, 0.0 us)
Async XLA Ops:
  7.2 1.5 copy-start
  7.2 182.6 %all-gather.5.cloned.1.call-start = ((), (), s32[]{:S(2)}) async-start(), calls=%async_computation.3 | async-start | bytes 2162688 | tf_op jit(solution)/shard_map/all_gather | solution.py:41
  7.9 185.5 %all-gather.3.cloned.1.call-start = ((), (), s32[]{:S(2)}) async-start(), calls=%async_computation.1 | async-start | bytes 4456448 | tf_op jit(solution)/shard_map/all_gather | solution.py:19
  8.7 294.3 %all-reduce.3.cloned.1.call-start = ((), (), s32[]{:S(2)}) async-start(), calls=%async_computation.4 | async-start | bytes 655360 | tf_op jit(solution)/shard_map/psum | solution.py:62
  9.6 6.2 %collective-permute-start = (f32[128,64]{0,1:T(8,128)S(1)}, f32[128,64]{0,1:T(8,128)S(1)}, u32[]{:S(2)}, u32[]{:S(2)}) collective-permute-start(f32[128,64]{0,1:T(8,128)S(1)} %fusion.54), channel_id=1, source_target_pairs={{0,16},{16,0},{32,48},{48,32},{64,80},{80,64},{96,112},{112,96},{1... | collective-permute-start | bytes 98312 | tf_op jit(solution)/shard_map/ppermute | solution.py:17
  15.8 8.0 %collective-permute-start.1 = (f32[128,64]{0,1:T(8,128)S(1)}, f32[128,64]{0,1:T(8,128)S(1)}, u32[]{:S(2)}, u32[]{:S(2)}) collective-permute-start(f32[128,64]{0,1:T(8,128)S(1)} %add.91), channel_id=1, source_target_pairs={{0,32},{16,48},{32,0},{48,16},{64,96},{80,112},{96,64},{112,80},{1... | collective-permute-start | bytes 98312 | tf_op jit(solution)/shard_map/ppermute | solution.py:17
  23.8 150.6 %collective-permute-start.2 = (f32[128,64]{0,1:T(8,128)S(1)}, f32[128,64]{0,1:T(8,128)S(1)}, u32[]{:S(2)}, u32[]{:S(2)}) collective-permute-start(f32[128,64]{0,1:T(8,128)S(1)} %add.92), channel_id=1, source_target_pairs={{0,64},{16,80},{32,96},{48,112},{64,0},{80,16},{96,32},{112,48},{1... | collective-permute-start | bytes 98312 | tf_op jit(solution)/shard_map/ppermute | solution.py:17
  174.4 5.8 %collective-permute-start.3 = (f32[128,64]{0,1:T(8,128)S(1)}, f32[128,64]{0,1:T(8,128)S(1)}, u32[]{:S(2)}, u32[]{:S(2)}) collective-permute-start(f32[128,64]{0,1:T(8,128)S(1)} %add.93), channel_id=1, source_target_pairs={{0,128},{16,144},{32,160},{48,176},{64,192},{80,208},{96,224},{112... | collective-permute-start | bytes 98312 | tf_op jit(solution)/shard_map/ppermute | solution.py:17
  180.2 7.9 %collective-permute-start.4 = (f32[128,64]{0,1:T(8,128)S(1)}, f32[128,64]{0,1:T(8,128)S(1)}, u32[]{:S(2)}, u32[]{:S(2)}) collective-permute-start(f32[128,64]{0,1:T(8,128)S(1)} %add.94), channel_id=1, source_target_pairs={{0,256},{16,272},{32,288},{48,304},{64,320},{80,336},{96,352},{112... | collective-permute-start | bytes 98312 | tf_op jit(solution)/shard_map/ppermute | solution.py:17
  193.3 3.0 copy-start.2
  193.3 340.9 %reduce-scatter.2.cloned.1.call-start = ((), (), s32[]{:S(2)}) async-start(), calls=%async_computation.2 | async-start | bytes 2162688 | tf_op jit(solution)/shard_map/reduce_scatter | solution.py:33
  196.7 110.8 %copy-start.1 = (bf16[128,8192]{1,0:T(8,128)(2,1)S(1)}, bf16[128,8192]{1,0:T(8,128)(2,1)}, u32[]{:S(2)}) copy-start(bf16[128,8192]{1,0:T(8,128)(2,1)} %all-gather.5.cloned.1.call-done) | copy-start | bytes 6291460
  198.4 113.3 %copy-start.3 = (bf16[256,64]{0,1:T(8,128)(2,1)S(1)}, bf16[256,64]{0,1:T(8,128)(2,1)}, u32[]{:S(2)}) copy-start(bf16[256,64]{0,1:T(8,128)(2,1)} %param.13) | copy-start | bytes 98308
  198.4 335.8 %copy-start.4 = (bf16[64,256]{1,0:T(8,128)(2,1)S(1)}, bf16[64,256]{1,0:T(8,128)(2,1)}, u32[]{:S(2)}) copy-start(bf16[64,256]{1,0:T(8,128)(2,1)} %param.14) | copy-start | bytes 98308
Sparse Core Ops, SparseCore 0:
  11.0 85.4 all-gather.4
  98.6 43.2 all-gather.2
  193.4 109.4 all-reduce.2
  307.2 226.9 reduce-scatter.1
